TPU v7x, 32 devices: a whole 2x2x4 slice. The times are simulated.
32 devices in a mesh: dp: 8 (over z, x), tensor: 4 (over y, core).
Axes of the slice: x: 2, y: 2, z: 4, core: 2. Of those that a mesh axis runs over, the one named last changes fastest.
Arguments:
- clip_tokens: bfloat16 [8, 1568, 768], P('dp', 'tensor'), as said below
- time_qkv: bfloat16 [3, 768, 768], P(None, 'dp', 'tensor'), may hold values from -0.21875 to 0.21875
- time_out: bfloat16 [768, 768], P('tensor', 'dp'), may hold values from -0.625 to 0.625
- time_mixer: bfloat16 [768, 768], P(('dp', 'tensor')), may hold values from -0.21875 to 0.21875
- space_qkv: bfloat16 [3, 768, 768], P(None, 'dp', 'tensor'), may hold values from -0.21875 to 0.21875
- space_out: bfloat16 [768, 768], P('tensor', 'dp'), may hold values from -3.5 to 3.5
- hidden_in: bfloat16 [768, 3072], P('dp', 'tensor'), may hold values from -0.21875 to 0.21875
- hidden_out: bfloat16 [3072, 768], P('tensor', 'dp'), may hold values from -0.109375 to 0.109375
- norm_gain: bfloat16 [3, 768], P(None, ('dp', 'tensor')), may hold values from 0.25 to 1.75
- norm_bias: bfloat16 [3, 768], P(None, ('dp', 'tensor')), may hold values from -3 to 3
- cotangent: bfloat16 [8, 1568, 768], P('dp', 'tensor'), may hold values from -6 to 6
Outputs:
- block_out: float32 [8, 1568, 768], P('dp', 'tensor')
- input_grad: float32 [8, 1568, 768], P('dp', 'tensor')
- time_qkv_grad: float32 [3, 768, 768], P(None, 'dp', 'tensor')
- time_out_grad: float32 [768, 768], P('tensor', 'dp')
- time_mixer_grad: float32 [768, 768], P(('dp', 'tensor'))
- space_qkv_grad: float32 [3, 768, 768], P(None, 'dp', 'tensor')
- space_out_grad: float32 [768, 768], P('tensor', 'dp')
- hidden_in_grad: float32 [768, 3072], P('dp', 'tensor')
- hidden_out_grad: float32 [3072, 768], P('tensor', 'dp')
- gain_grad: float32 [3, 768], P(None, ('dp', 'tensor'))
- bias_grad: float32 [3, 768], P(None, ('dp', 'tensor'))
- qk_clip: float32 [2, 12], P(None, 'tensor')
Inputs may be any that keep to these rules, and one draw needn't show every extreme that they name: `clip_tokens`: 8 clips of tokens of order one.
All inputs are finite; a program needn't handle non-finite values.
Results may differ from a plain program's by a relative error of at most 0.035.
Values may be sent and summed in bfloat16 or wider, within the bound.
No kernel may reach another device: no remote copies, remote signals or barrier semaphores. Data moves between devices by JAX's collectives and lax.ppermute only.
A program may use at most 128 MiB of HBM per device.

v0:
```python
import jax
import jax.numpy as jnp
from jax import lax
from jax.sharding import PartitionSpec as P

HD = 64
FRAMES = 8
PATCHES = 196


SCALE = 0.125
TAU = 2.0
EPS = 1e-06
TIME_FORMS = ("cfphe,cgphe->cphfg", "cphfg,cgphe->cfphe", "cphfg,cfphe->cgphe")
SPACE_FORMS = ("cfphe,cfqhe->cfhpq", "cfhpq,cfqhe->cfphe", "cfhpq,cfphe->cfqhe")


def matmul(form, left, right):
    return jnp.einsum(form, left, right, preferred_element_type=jnp.float32)


def gelu_exact(values):
    return jax.nn.gelu(values, approximate=False)


def normalize(row_block, gain_row, bias_row):
    row_mean = jnp.mean(row_block, axis=-1, keepdims=True)
    centered = row_block - row_mean
    inverse = lax.rsqrt(jnp.mean(centered * centered, axis=-1, keepdims=True) + EPS)
    scaled = centered * inverse
    return (scaled, inverse, (scaled * gain_row + bias_row).astype(jnp.bfloat16))


def norm_backward(grad_normed, scaled, inverse, gain_row):
    weighted = grad_normed * gain_row
    return inverse * (
        weighted
        - jnp.mean(weighted, axis=-1, keepdims=True)
        - scaled * jnp.mean(weighted * scaled, axis=-1, keepdims=True)
    )


def gather_rows(local_rows):
    return lax.all_gather(local_rows, "tensor", axis=1, tiled=True)


def scatter_rows(partial_term):
    return lax.psum_scatter(
        partial_term.astype(jnp.bfloat16), "tensor", scatter_dimension=1, tiled=True
    ).astype(jnp.float32)


def gather_grads(local_grad):
    return lax.all_gather(local_grad, "tensor", axis=1, tiled=True)


def scatter_grads(partial_term):
    return lax.psum_scatter(
        partial_term.astype(jnp.bfloat16), "tensor", scatter_dimension=1, tiled=True
    ).astype(jnp.float32)


def recall(local_rows):
    again_rows = lax.all_gather(local_rows, "tensor", axis=1, tiled=True)
    return again_rows


def fetch_attn(weight_qkv, weight_out):
    return (
        lax.all_gather(weight_qkv, "dp", axis=1, tiled=True),
        lax.all_gather(weight_out, "dp", axis=1, tiled=True),
    )


def refetch_attn(weight_qkv, weight_out):
    fetched = (
        lax.all_gather(weight_qkv, "dp", axis=1, tiled=True),
        lax.all_gather(weight_out, "dp", axis=1, tiled=True),
    )
    return fetched


def fetch_hidden(weight_in, weight_out):
    return (
        lax.all_gather(weight_in, "dp", axis=0, tiled=True),
        lax.all_gather(weight_out, "dp", axis=1, tiled=True),
    )


def refetch_hidden(weight_in, weight_out):
    fetched = (
        lax.all_gather(weight_in, "dp", axis=0, tiled=True),
        lax.all_gather(weight_out, "dp", axis=1, tiled=True),
    )
    return fetched


def return_attn(grad_qkv, grad_out):
    return (
        lax.psum_scatter(grad_qkv, "dp", scatter_dimension=1, tiled=True),
        lax.psum_scatter(grad_out, "dp", scatter_dimension=1, tiled=True),
    )


def return_hidden(grad_in, grad_out):
    return (
        lax.psum_scatter(grad_in, "dp", scatter_dimension=0, tiled=True),
        lax.psum_scatter(grad_out, "dp", scatter_dimension=1, tiled=True),
    )


def heads_forward(hidden, weight_qkv, forms):
    clip_count, seq_len, width = hidden.shape
    group_width = weight_qkv.shape[2]
    heads_loc = group_width // HD
    projected = matmul("csd,ndk->ncsk", hidden, weight_qkv).astype(jnp.bfloat16)
    shaped = projected.reshape(3, clip_count, FRAMES, PATCHES, heads_loc, HD)
    logits = matmul(forms[0], shaped[0], shaped[1]) * SCALE
    row_peak = jnp.max(logits, axis=-1, keepdims=True)
    exponent = jnp.exp(logits - row_peak)
    row_total = jnp.sum(exponent, axis=-1, keepdims=True)
    log_total = row_peak + jnp.log(row_total)
    weights = (exponent / row_total).astype(jnp.bfloat16)
    mixed_heads = matmul(forms[1], weights, shaped[2]).astype(jnp.bfloat16)
    mixed_heads = mixed_heads.reshape(clip_count, seq_len, group_width)
    highest = jnp.max(logits, axis=(0, 1, 3, 4))
    return (shaped, log_total, mixed_heads, highest)


def heads_backward(shaped, log_total, grad_mixed, forms):
    grad_shaped = grad_mixed.reshape(shaped.shape[1:])
    logits = matmul(forms[0], shaped[0], shaped[1]) * SCALE
    weights = jnp.exp(logits - log_total)
    grad_weights = matmul(forms[0], grad_shaped, shaped[2])
    grad_values = matmul(forms[2], weights.astype(jnp.bfloat16), grad_shaped)
    row_inner = jnp.sum(grad_weights * weights, axis=-1, keepdims=True)
    grad_logits = (weights * (grad_weights - row_inner)).astype(jnp.bfloat16)
    grad_query = matmul(forms[1], grad_logits, shaped[1]) * SCALE
    grad_keys = matmul(forms[2], grad_logits, shaped[0]) * SCALE
    stacked = jnp.stack([grad_query, grad_keys, grad_values]).astype(jnp.bfloat16)
    return stacked.reshape(3, grad_mixed.shape[0], grad_mixed.shape[1], grad_mixed.shape[2])


def attention_back(
    grad_local, local_rows, shaped, log_total, mixed_heads, weight_qkv, weight_out, forms
):
    grad_full = gather_grads(grad_local)
    grad_wout = matmul("csk,csd->kd", mixed_heads, grad_full)
    grad_mixed = matmul("csd,kd->csk", grad_full, weight_out).astype(jnp.bfloat16)
    grad_qkv = heads_backward(shaped, log_total, grad_mixed, forms)
    hidden = recall(local_rows)
    grad_wqkv = matmul("csd,ncsk->ndk", hidden, grad_qkv)
    grad_hidden = scatter_grads(matmul("ncsk,ndk->csd", grad_qkv, weight_qkv))
    return (grad_hidden, grad_wqkv, grad_wout)


def row_sums(grad_normed, scaled):
    return (jnp.sum(grad_normed * scaled, axis=(0, 1)), jnp.sum(grad_normed, axis=(0, 1)))


def shards(
    clip_tokens,
    time_qkv,
    time_out,
    time_mixer,
    space_qkv,
    space_out,
    hidden_in,
    hidden_out,
    norm_gain,
    norm_bias,
    cotangent,
):
    mixer_full, gain_rows, bias_rows = (
        lax.all_gather(time_mixer, ("dp", "tensor"), axis=0, tiled=True),
        lax.all_gather(norm_gain, ("dp", "tensor"), axis=1, tiled=True),
        lax.all_gather(norm_bias, ("dp", "tensor"), axis=1, tiled=True),
    )
    gain_rows = gain_rows.astype(jnp.float32)
    bias_rows = bias_rows.astype(jnp.float32)
    tokens = clip_tokens.astype(jnp.float32)
    qkv_time, out_time = fetch_attn(time_qkv, time_out)
    scaled_one, inverse_one, low_one = normalize(tokens, gain_rows[0], bias_rows[0])
    full_one = gather_rows(low_one)
    shaped_one, lse_one, mixed_one, high_one = heads_forward(full_one, qkv_time, TIME_FORMS)
    mixer_in = scatter_rows(matmul("csk,kd->csd", mixed_one, out_time)).astype(jnp.bfloat16)
    after_time = tokens + matmul("csd,de->cse", mixer_in, mixer_full)
    qkv_space, out_space = fetch_attn(space_qkv, space_out)
    scaled_two, inverse_two, low_two = normalize(after_time, gain_rows[1], bias_rows[1])
    full_two = gather_rows(low_two)
    shaped_two, lse_two, mixed_two, high_two = heads_forward(full_two, qkv_space, SPACE_FORMS)
    after_space = after_time + scatter_rows(matmul("csk,kd->csd", mixed_two, out_space))
    weight_up, weight_down = fetch_hidden(hidden_in, hidden_out)
    scaled_three, inverse_three, low_three = normalize(after_space, gain_rows[2], bias_rows[2])
    full_three = gather_rows(low_three)
    pre_gelu = matmul("csd,df->csf", full_three, weight_up)
    active = gelu_exact(pre_gelu).astype(jnp.bfloat16)
    block_out = after_space + scatter_rows(matmul("csf,fd->csd", active, weight_down))
    highest = lax.pmax(jnp.stack([high_one, high_two]), "dp")
    qk_clip = jnp.sqrt(TAU / jnp.maximum(highest, TAU))
    back_up, back_down = refetch_hidden(hidden_in, hidden_out)
    grad_full = gather_grads(cotangent)
    grad_down = matmul("csf,csd->fd", active, grad_full)
    grad_active = matmul("csd,fd->csf", grad_full, back_down)
    gelu_value, gelu_pull = jax.vjp(gelu_exact, pre_gelu)
    grad_pre = gelu_pull(grad_active)[0].astype(jnp.bfloat16)
    hidden_three = recall(low_three)
    grad_up = matmul("csd,csf->df", hidden_three, grad_pre)
    grad_low_three = scatter_grads(matmul("csf,df->csd", grad_pre, back_up))
    hidden_in_grad, hidden_out_grad = return_hidden(grad_up, grad_down)
    gain_three, bias_three = row_sums(grad_low_three, scaled_three)
    grad_after_space = cotangent.astype(jnp.float32) + norm_backward(
        grad_low_three, scaled_three, inverse_three, gain_rows[2]
    )
    back_qkv_space, back_out_space = refetch_attn(space_qkv, space_out)
    grad_low_two, grad_sqkv, grad_sout = attention_back(
        grad_after_space.astype(jnp.bfloat16),
        low_two,
        shaped_two,
        lse_two,
        mixed_two,
        back_qkv_space,
        back_out_space,
        SPACE_FORMS,
    )
    space_qkv_grad, space_out_grad = return_attn(grad_sqkv, grad_sout)
    gain_two, bias_two = row_sums(grad_low_two, scaled_two)
    grad_after_time = grad_after_space + norm_backward(
        grad_low_two, scaled_two, inverse_two, gain_rows[1]
    )
    grad_mixer_out = grad_after_time.astype(jnp.bfloat16)
    grad_mixer = matmul("csd,cse->de", mixer_in, grad_mixer_out)
    grad_mixer_in = matmul("cse,de->csd", grad_mixer_out, mixer_full).astype(jnp.bfloat16)
    back_qkv_time, back_out_time = refetch_attn(time_qkv, time_out)
    grad_low_one, grad_tqkv, grad_tout = attention_back(
        grad_mixer_in,
        low_one,
        shaped_one,
        lse_one,
        mixed_one,
        back_qkv_time,
        back_out_time,
        TIME_FORMS,
    )
    time_qkv_grad, time_out_grad = return_attn(grad_tqkv, grad_tout)
    gain_one, bias_one = row_sums(grad_low_one, scaled_one)
    input_grad = grad_after_time + norm_backward(
        grad_low_one, scaled_one, inverse_one, gain_rows[0]
    )
    gain_terms = jnp.stack([gain_one, gain_two, gain_three])
    bias_terms = jnp.stack([bias_one, bias_two, bias_three])
    time_mixer_grad, gain_grad, bias_grad = (
        lax.psum_scatter(grad_mixer, ("dp", "tensor"), scatter_dimension=0, tiled=True),
        lax.psum_scatter(gain_terms, ("dp", "tensor"), scatter_dimension=1, tiled=True),
        lax.psum_scatter(bias_terms, ("dp", "tensor"), scatter_dimension=1, tiled=True),
    )
    return (
        block_out,
        input_grad,
        time_qkv_grad,
        time_out_grad,
        time_mixer_grad,
        space_qkv_grad,
        space_out_grad,
        hidden_in_grad,
        hidden_out_grad,
        gain_grad,
        bias_grad,
        qk_clip,
    )


def solution(mesh):
    in_specs = (
        P("dp", "tensor", None),
        P(None, "dp", "tensor"),
        P("tensor", "dp"),
        P(("dp", "tensor"), None),
        P(None, "dp", "tensor"),
        P("tensor", "dp"),
        P("dp", "tensor"),
        P("tensor", "dp"),
        P(None, ("dp", "tensor")),
        P(None, ("dp", "tensor")),
        P("dp", "tensor", None),
    )
    out_specs = (
        P("dp", "tensor", None),
        P("dp", "tensor", None),
        P(None, "dp", "tensor"),
        P("tensor", "dp"),
        P(("dp", "tensor"), None),
        P(None, "dp", "tensor"),
        P("tensor", "dp"),
        P("dp", "tensor"),
        P("tensor", "dp"),
        P(None, ("dp", "tensor")),
        P(None, ("dp", "tensor")),
        P(None, "tensor"),
    )
    return jax.shard_map(shards, mesh=mesh, in_specs=in_specs, out_specs=out_specs, check_vma=False)
```

profile of v0, /device:TPU:0, one launch (start us, length us, event | category | flops | bytes accessed | tf_op | source)
XLA Modules:
  0.0 1217.1 jit_solution(4882895162532141707)
XLA Ops:
  10.8 43.5 %all-gather.1 = bf16[32,24,3]{1,2,0:T(4,128)(2,1)S(1)} all-gather(bf16[1,24,3]{1,2,0:T(4,128)(2,1)} %bitcast.275), channel_id=1, replica_groups=mesh['dp'=8,'tensor'=4] {'dp','tensor'}, dimensions={0}, use_global_device_ids=true | all-gather | bytes 4752 | tf_op jit(solution)/shard_map/all_gather | solution.py:176
  54.6 36.9 %all-gather.2 = bf16[32,24,3]{1,2,0:T(4,128)(2,1)S(1)} all-gather(bf16[1,24,3]{1,2,0:T(4,128)(2,1)} %bitcast.276), channel_id=1, replica_groups=mesh['dp'=8,'tensor'=4] {'dp','tensor'}, dimensions={0}, use_global_device_ids=true | all-gather | bytes 4752 | tf_op jit(solution)/shard_map/all_gather | solution.py:177
  95.1 31.1 %all_gather.58 = bf16[192,768]{0,1:T(8,128)(2,1)S(1)} all-gather(bf16[192,96]{0,1:T(8,128)(2,1)S(1)} %copy.142), channel_id=1, replica_groups=mesh['dp'=8,'tensor'=4] {'dp'}, dimensions={1}, use_global_device_ids=true | all-gather | bytes 331776 | tf_op jit(solution)/shard_map/all_gather | solution.py:71
  126.2 39.0 %all_gather.57 = bf16[3,768,192]{2,0,1:T(4,128)(2,1)S(1)} all-gather(bf16[3,96,192]{2,0,1:T(4,128)(2,1)S(1)} %copy.135), channel_id=1, replica_groups=mesh['dp'=8,'tensor'=4] {'dp'}, dimensions={1}, use_global_device_ids=true | all-gather | bytes 995328 | tf_op jit(solution)/shard_map/all_gather | solution.py:70
  199.1 30.4 %reduce-scatter.24.cloned.1.call-done = bf16[1,392,768]{2,1,0:T(8,128)(2,1)} async-done(((bf16[1,1568,768]{2,1,0:T(8,128)(2,1)}), bf16[1,392,768]{2,1,0:T(8,128)(2,1)}) %reduce-scatter.24.cloned.1.call-update) | async-done | bytes 602128 | tf_op jit(solution)/shard_map/reduce_scatter | solution.py:48
  234.2 38.7 %all_gather.61 = bf16[3,768,192]{2,0,1:T(4,128)(2,1)} all-gather(bf16[3,96,192]{2,0,1:T(4,128)(2,1)S(1)} %copy.143), channel_id=1, replica_groups=mesh['dp'=8,'tensor'=4] {'dp'}, dimensions={1}, use_global_device_ids=true | all-gather | bytes 995328 | tf_op jit(solution)/shard_map/all_gather | solution.py:70
  275.6 33.1 %all_gather.62 = bf16[192,768]{0,1:T(8,128)(2,1)} all-gather(bf16[192,96]{0,1:T(8,128)(2,1)S(1)} %copy.150), channel_id=1, replica_groups=mesh['dp'=8,'tensor'=4] {'dp'}, dimensions={1}, use_global_device_ids=true | all-gather | bytes 331776 | tf_op jit(solution)/shard_map/all_gather | solution.py:71
  333.5 32.2 %reduce-scatter.26.cloned.1.call-done = bf16[1,392,768]{2,1,0:T(8,128)(2,1)} async-done(((bf16[1,1568,768]{2,1,0:T(8,128)(2,1)}), bf16[1,392,768]{2,1,0:T(8,128)(2,1)}) %reduce-scatter.26.cloned.1.call-update) | async-done | bytes 602128 | tf_op jit(solution)/shard_map/reduce_scatter | solution.py:48
  376.1 24.1 %all-gather.19.cloned.1.call-done = bf16[1,1568,768]{2,1,0:T(8,128)(2,1)} async-done(((bf16[1,392,768]{2,1,0:T(8,128)(2,1)}), bf16[1,1568,768]{2,1,0:T(8,128)(2,1)}) %all-gather.19.cloned.1.call-update) | async-done | bytes 2408464 | tf_op jit(solution)/shard_map/all_gather | solution.py:44
  415.6 28.3 %all-gather.23.cloned.1.call-done = bf16[768,768]{0,1:T(8,128)(2,1)} async-done(((bf16[768,96]{0,1:T(8,128)(2,1)}), bf16[768,768]{0,1:T(8,128)(2,1)}) %all-gather.23.cloned.1.call-update) | async-done | bytes 1179664 | tf_op jit(solution)/shard_map/all_gather | solution.py:86
  443.9 24.3 %all-gather.25.cloned.1.call-done = bf16[1,1568,768]{2,1,0:T(8,128)(2,1)} async-done(((bf16[1,392,768]{2,1,0:T(8,128)(2,1)}), bf16[1,1568,768]{2,1,0:T(8,128)(2,1)}) %all-gather.25.cloned.1.call-update) | async-done | bytes 2408464 | tf_op jit(solution)/shard_map/all_gather | solution.py:54
  486.9 27.8 %reduce-scatter.30.cloned.1.call-done = bf16[1,392,768]{2,1,0:T(8,128)(2,1)} async-done(((bf16[1,1568,768]{2,1,0:T(8,128)(2,1)}), bf16[1,392,768]{2,1,0:T(8,128)(2,1)}) %reduce-scatter.30.cloned.1.call-update) | async-done | bytes 602128 | tf_op jit(solution)/shard_map/reduce_scatter | solution.py:58
  516.8 34.0 %reduce-scatter.28.cloned.1.call-done = bf16[1,392,768]{2,1,0:T(8,128)(2,1)} async-done(((bf16[1,1568,768]{2,1,0:T(8,128)(2,1)}), bf16[1,392,768]{2,1,0:T(8,128)(2,1)}) %reduce-scatter.28.cloned.1.call-update) | async-done | bytes 602128 | tf_op jit(solution)/shard_map/reduce_scatter | solution.py:48
  554.7 24.4 %all-gather.27.cloned.1.call-done = bf16[1,1568,768]{2,1,0:T(8,128)(2,1)} async-done(((bf16[1,392,768]{2,1,0:T(8,128)(2,1)}), bf16[1,1568,768]{2,1,0:T(8,128)(2,1)}) %all-gather.27.cloned.1.call-update) | async-done | bytes 2408464 | tf_op jit(solution)/shard_map/all_gather | solution.py:54
  613.8 32.9 %reduce-scatter.32.cloned.1.call-done = bf16[1,392,768]{2,1,0:T(8,128)(2,1)} async-done(((bf16[1,1568,768]{2,1,0:T(8,128)(2,1)}), bf16[1,392,768]{2,1,0:T(8,128)(2,1)}) %reduce-scatter.32.cloned.1.call-update) | async-done | bytes 602128 | tf_op jit(solution)/shard_map/reduce_scatter | solution.py:58
  749.7 39.7 %reduce-scatter.46.cloned.1.call-done = f32[96,576]{1,0:T(8,128)} async-done(((f32[768,576]{1,0:T(8,128)}), f32[96,576]{1,0:T(8,128)}) %reduce-scatter.46.cloned.1.call-update) | async-done | bytes 221200
  791.3 19.4 %pmax.7 = f32[2,3]{1,0:T(2,128)S(1)} all-reduce(f32[2,3]{1,0:T(2,128)S(1)} %pad_maximum_fusion.2), channel_id=1, replica_groups=mesh['dp'=8,'tensor'=4] {'dp'}, use_global_device_ids=true, to_apply=%region_41.0 | all-reduce | flops 6 | bytes 48 | tf_op jit(solution)/shard_map/pmax | solution.py:199
  811.2 44.2 %reduce-scatter.44.cloned.1.call-done = f32[96,192]{1,0:T(8,128)} async-done(((f32[768,192]{1,0:T(8,128)}), f32[96,192]{1,0:T(8,128)}) %reduce-scatter.44.cloned.1.call-update) | async-done | bytes 73744
  857.1 67.5 %reduce-scatter.42.cloned.1.call-done = f32[96,576]{1,0:T(8,128)} async-done(((f32[768,576]{1,0:T(8,128)}), f32[96,576]{1,0:T(8,128)}) %reduce-scatter.42.cloned.1.call-update) | async-done | bytes 221200
  926.5 33.3 %reduce-scatter.34.cloned.1.call-done = bf16[1,392,768]{2,1,0:T(8,128)(2,1)} async-done(((bf16[1,1568,768]{2,1,0:T(8,128)(2,1)}), bf16[1,392,768]{2,1,0:T(8,128)(2,1)}) %reduce-scatter.34.cloned.1.call-update) | async-done | bytes 602128 | tf_op jit(solution)/shard_map/reduce_scatter | solution.py:58
  961.6 41.4 %all-reduce.2 = (f32[3,768]{1,0:T(4,128)S(1)}, f32[3,768]{1,0:T(4,128)S(1)}) all-reduce(f32[3,768]{1,0:T(4,128)S(1)} %pad_maximum_fusion, f32[3,768]{1,0:T(4,128)S(1)} %pad_maximum_fusion.1), channel_id=16, replica_groups=mesh['dp'=8,'tensor'=4] {'dp','tensor'}, use_global_device_ids=true, to_apply=%region_34.0.clone | all-reduce | flops 4608 | bytes 36864
  1006.9 26.4 %reduce-scatter.38.cloned.1.call-done = f32[96,768]{1,0:T(8,128)} async-done(((f32[768,768]{1,0:T(8,128)}), f32[96,768]{1,0:T(8,128)}) %reduce-scatter.38.cloned.1.call-update) | async-done | bytes 294928 | tf_op jit(solution)/shard_map/reduce_scatter | solution.py:107
  1033.3 72.1 %reduce-scatter.40.cloned.1.call-done = f32[768,96]{0,1:T(8,128)} async-done(((f32[768,768]{0,1:T(8,128)}), f32[768,96]{0,1:T(8,128)}) %reduce-scatter.40.cloned.1.call-update) | async-done | bytes 294928 | tf_op jit(solution)/shard_map/reduce_scatter | solution.py:108
  1105.4 103.9 %reduce-scatter.36.cloned.1.call-done = f32[24,768]{1,0:T(8,128)} async-done(((f32[768,768]{1,0:T(8,128)}), f32[24,768]{1,0:T(8,128)}) %reduce-scatter.36.cloned.1.call-update) | async-done | bytes 73744 | tf_op jit(solution)/shard_map/reduce_scatter | solution.py:253
  (295 shorter events, 271.4 us)
Async XLA Ops:
  8.0 159.2 %all-gather.13.cloned.1.call-start = ((), (), s32[]{:S(2)}) async-start(), calls=%async_computation.13 | async-start | bytes 3010560 | tf_op jit(solution)/shard_map/all_gather | solution.py:44
  94.1 105.0 %all-gather.15.cloned.1.call-start = ((), (), s32[]{:S(2)}) async-start(), calls=%async_computation.15 | async-start | bytes 1216512 | tf_op jit(solution)/shard_map/all_gather | solution.py:175
  94.8 134.7 %reduce-scatter.24.cloned.1.call-start = ((), (), s32[]{:S(2)}) async-start(), calls=%async_computation.14 | async-start | bytes 3010560 | tf_op jit(solution)/shard_map/reduce_scatter | solution.py:48
  198.6 110.0 %all-gather.17.cloned.1.call-start = ((), (), s32[]{:S(2)}) async-start(), calls=%async_computation.16 | async-start | bytes 3010560 | tf_op jit(solution)/shard_map/all_gather | solution.py:44
  233.9 131.7 %reduce-scatter.26.cloned.1.call-start = ((), (), s32[]{:S(2)}) async-start(), calls=%async_computation.17 | async-start | bytes 3010560 | tf_op jit(solution)/shard_map/reduce_scatter | solution.py:48
  332.8 43.3 %all-gather.21.cloned.1.call-start = ((), (), s32[]{:S(2)}) async-start(), calls=%async_computation.19 | async-start | bytes 1327104 | tf_op jit(solution)/shard_map/all_gather | solution.py:85
  333.4 66.9 %all-gather.19.cloned.1.call-start = ((), (), s32[]{:S(2)}) async-start(), calls=%async_computation.18 | async-start | bytes 3010560 | tf_op jit(solution)/shard_map/all_gather | solution.py:44
  369.4 74.4 %all-gather.23.cloned.1.call-start = ((), (), s32[]{:S(2)}) async-start(), calls=%async_computation.20 | async-start | bytes 1327104 | tf_op jit(solution)/shard_map/all_gather | solution.py:86
  370.0 98.2 %all-gather.25.cloned.1.call-start = ((), (), s32[]{:S(2)}) async-start(), calls=%async_computation.22 | async-start | bytes 3010560 | tf_op jit(solution)/shard_map/all_gather | solution.py:54
  370.8 144.0 %reduce-scatter.30.cloned.1.call-start = ((), (), s32[]{:S(2)}) async-start(), calls=%async_computation.23 | async-start | bytes 3010560 | tf_op jit(solution)/shard_map/reduce_scatter | solution.py:58
  481.3 69.5 %reduce-scatter.28.cloned.1.call-start = ((), (), s32[]{:S(2)}) async-start(), calls=%async_computation.21 | async-start | bytes 3010560 | tf_op jit(solution)/shard_map/reduce_scatter | solution.py:48
  486.9 92.2 %all-gather.27.cloned.1.call-start = ((), (), s32[]{:S(2)}) async-start(), calls=%async_computation.24 | async-start | bytes 3010560 | tf_op jit(solution)/shard_map/all_gather | solution.py:54
  554.6 92.1 %reduce-scatter.32.cloned.1.call-start = ((), (), s32[]{:S(2)}) async-start(), calls=%async_computation.25 | async-start | bytes 3010560 | tf_op jit(solution)/shard_map/reduce_scatter | solution.py:58
  613.4 64.7 %all-gather.29.cloned.1.call-start = ((), (), s32[]{:S(2)}) async-start(), calls=%async_computation.30 | async-start | bytes 3010560 | tf_op jit(solution)/shard_map/all_gather | solution.py:54
  653.6 94.5 %reduce-scatter.48.cloned.1.call-start = ((), (), s32[]{:S(2)}) async-start(), calls=%async_computation.34 | async-start | bytes 884736
  657.3 132.1 %reduce-scatter.46.cloned.1.call-start = ((), (), s32[]{:S(2)}) async-start(), calls=%async_computation.33 | async-start | bytes 2211840
  671.7 183.7 %reduce-scatter.44.cloned.1.call-start = ((), (), s32[]{:S(2)}) async-start(), calls=%async_computation.32 | async-start | bytes 884736
  713.9 210.7 %reduce-scatter.42.cloned.1.call-start = ((), (), s32[]{:S(2)}) async-start(), calls=%async_computation.31 | async-start | bytes 2211840
  725.7 234.1 %reduce-scatter.34.cloned.1.call-start = ((), (), s32[]{:S(2)}) async-start(), calls=%async_computation.26 | async-start | bytes 3010560 | tf_op jit(solution)/shard_map/reduce_scatter | solution.py:58
  730.8 302.5 %reduce-scatter.38.cloned.1.call-start = ((), (), s32[]{:S(2)}) async-start(), calls=%async_computation.28 | async-start | bytes 2654208 | tf_op jit(solution)/shard_map/reduce_scatter | solution.py:107
  737.9 367.5 %reduce-scatter.40.cloned.1.call-start = ((), (), s32[]{:S(2)}) async-start(), calls=%async_computation.29 | async-start | bytes 2654208 | tf_op jit(solution)/shard_map/reduce_scatter | solution.py:108
  744.2 465.0 %reduce-scatter.36.cloned.1.call-start = ((), (), s32[]{:S(2)}) async-start(), calls=%async_computation.27 | async-start | bytes 2433024 | tf_op jit(solution)/shard_map/reduce_scatter | solution.py:253
  747.9 211.8 %copy-start.42 = (f32[392]{0:T(512)S(1)}, f32[392]{0:T(512)}, u32[]{:S(2)}) copy-start(f32[392]{0:T(512)} %copy-done.41) | copy-start | bytes 4708
  747.9 211.8 %copy-start.46 = (f32[392]{0:T(512)S(1)}, f32[392]{0:T(512)}, u32[]{:S(2)}) copy-start(f32[392]{0:T(512)} %copy-done.45) | copy-start | bytes 4708
  (51 other events, 1332.6 us)
Sparse Core Ops, SparseCore 0:
  94.2 21.8 all-gather.12
  118.9 56.8 all-gather.14
  198.7 30.7 reduce-scatter.23
  234.1 24.3 all-gather.16
  333.0 32.6 reduce-scatter.25
  554.8 24.3 all-gather.26
  653.7 24.3 all-gather.28
Sparse Core Ops, SparseCore 1:
  335.5 40.6 all-gather.20
  377.6 22.7 all-gather.18
  402.3 41.5 all-gather.22
  445.5 22.7 all-gather.24
  481.4 33.3 reduce-scatter.29
  517.5 33.3 reduce-scatter.27
  613.5 33.2 reduce-scatter.31
  657.7 62.5 reduce-scatter.47
  723.6 65.7 reduce-scatter.45
  793.6 61.7 reduce-scatter.43
  858.8 65.7 reduce-scatter.41
  927.3 32.4 reduce-scatter.33
  963.7 69.6 reduce-scatter.37
  1037.4 67.9 reduce-scatter.39
  1111.3 97.9 reduce-scatter.35
where the time goes:
time: 1220 us
  waiting for transfers between devices  659 us (54%)
  blocking collectives  283 us (23%)
  matrix products  121 us (10%)
  local copies, waits for them, and re-layouts  105 us (9%)
  other arithmetic  30.1 us (2%)
  between operations  17.1 us (1%)
    unnamed x26, waiting for transfers between devices  154 us
    dot_general x29, matrix products, matmul(): return jnp.einsum(form, left, right, preferred_element_type=jnp.float32)  107 us
    reduce_scatter x1, waiting for transfers between devices, shards(): lax.psum_scatter(grad_mixer, ('dp', 'tensor'), scatter_dimension=0, tiled...  104 us
    reduce_scatter x3, waiting for transfers between devices, scatter_rows(): lax.psum_scatter(partial_term.astype(jnp.bfloat16), 'tensor', scatter_dim...  96.6 us
    reduce_scatter x3, waiting for transfers between devices, scatter_grads(): lax.psum_scatter(partial_term.astype(jnp.bfloat16), 'tensor', scatter_dim...  94 us
    all_gather x2, blocking collectives, fetch_attn(): lax.all_gather(weight_qkv, 'dp', axis=1, tiled=True)  77.7 us
    reduce_scatter x1, waiting for transfers between devices, return_hidden(): lax.psum_scatter(grad_out, 'dp', scatter_dimension=1, tiled=True)  72.1 us
    all_gather x2, blocking collectives, fetch_attn(): lax.all_gather(weight_out, 'dp', axis=1, tiled=True)  64.1 us
  transfers between devices with their start and end apart: 22, of which 18 were waited for; matrix products, arithmetic and copies ran while one was open for 13% of the time, Pallas kernels for 0%

commit v1 on v0

v1 whole, which is shorter than its diff:
```python
import functools

import jax
import jax.numpy as jnp
from jax import lax
from jax.experimental import pallas as pl
from jax.experimental.pallas import tpu as pltpu
from jax.sharding import PartitionSpec as P

HD = 64
FRAMES = 8
PATCHES = 196
PAD = 208
SCALE = 0.125
TAU = 2.0
EPS = 1e-06
AXES = ("dp", "tensor")
F32 = jnp.float32
BF16 = jnp.bfloat16
VMEM_LIMIT = 60 * 1024 * 1024


def place(z, x, y, c):
    return ((z * 2 + x) * 2 + y) * 2 + c


ALL = [(z, x, y, c) for z in range(4) for x in range(2) for y in range(2) for c in range(2)]


def pairs(move, keep=lambda z, x, y, c: True):
    return [(place(*i), place(*move(*i))) for i in ALL if keep(*i)]


SWAP_C = pairs(lambda z, x, y, c: (z, x, y, 1 - c))
SWAP_Y = pairs(lambda z, x, y, c: (z, x, 1 - y, c))
SWAP_YC = pairs(lambda z, x, y, c: (z, x, 1 - y, 1 - c))
SWAP_X = pairs(lambda z, x, y, c: (z, 1 - x, y, c))
SWAP_Z1 = pairs(lambda z, x, y, c: (z ^ 1, x, y, c))
SWAP_Z2 = pairs(lambda z, x, y, c: (z ^ 2, x, y, c))
Z_MID = pairs(lambda z, x, y, c: (3 - z, x, y, c), lambda z, x, y, c: z in (1, 2))
Z_OUT = pairs(lambda z, x, y, c: (z ^ 1, x, y, c), lambda z, x, y, c: z in (1, 2))
Z_IN = pairs(lambda z, x, y, c: (z ^ 1, x, y, c), lambda z, x, y, c: z in (0, 3))


def send(value, route):
    return lax.ppermute(value, AXES, route)


def dot_nn(a, b):
    return lax.dot_general(a, b, (((1,), (0,)), ((), ())), preferred_element_type=F32)


def dot_nt(a, b):
    return lax.dot_general(a, b, (((1,), (1,)), ((), ())), preferred_element_type=F32)


def dot_tn(a, b):
    return lax.dot_general(a, b, (((0,), (0,)), ((), ())), preferred_element_type=F32)


def group_at(step):
    return jnp.where(step < 2, 2 * step + 1, 2 * step - 4)


def piece_of(r, rx, slot):
    base = (r % 2) * 5
    if r < 2:
        return (base + rx, slot)
    if rx == 0:
        return (base + 2, slot)
    return (base + 3, slot) if slot < 2 else (base + 4, slot - 2)


def slot_rows(where_ref):
    z = where_ref[0]
    low = z < 2
    return [z, z ^ 1, jnp.where(low, 2, 1), jnp.where(low, 3, 0)]


def start_loads(torus, where_ref, pieces, stores, sems):
    if not torus:
        for r in range(4):
            for b in range(2):
                pltpu.make_async_copy(pieces[0].at[r, b], stores[b].at[r], sems.at[r, b]).start()
        return
    x = where_ref[1]
    zs = slot_rows(where_ref)
    for i in range(4):
        r = (1, 3, 0, 2)[i]
        for rx in range(2):
            for slot in range(4):
                which, lead = piece_of(r, rx, slot)
                row = pl.multiple_of((zs[slot] * 2 + (x ^ rx)) * 96, 96)
                for b in range(2):
                    pltpu.make_async_copy(
                        pieces[which].at[lead, pl.ds(b * 96, 96), :],
                        stores[b].at[r, pl.ds(row, 96), :],
                        sems.at[r, b],
                    ).start()


def wait_loads(r, stores, sems):
    for b in range(2):
        pltpu.make_async_copy(stores[b].at[r], stores[b].at[r], sems.at[r, b]).wait()


def out_slot(torus, where_ref, dp):
    if not torus:
        return dp
    z_to, x_to = dp // 2, dp % 2
    far = ((where_ref[0] >> 1) ^ (z_to // 2)) * 2
    return (where_ref[1] ^ x_to) * 4 + far + z_to % 2


def normed(rows):
    mean = jnp.mean(rows, axis=-1, keepdims=True)
    centered = rows - mean
    inverse = lax.rsqrt(jnp.mean(centered * centered, axis=-1, keepdims=True) + EPS)
    return centered * inverse, inverse


def norm_back(dh, scaled, inverse, gain):
    weighted = dh * gain
    return inverse * (
        weighted
        - jnp.mean(weighted, axis=-1, keepdims=True)
        - scaled * jnp.mean(weighted * scaled, axis=-1, keepdims=True)
    )


def norm_sums(dh, scaled):
    gain = jnp.sum(dh * scaled, axis=0, keepdims=True)
    bias = jnp.sum(dh, axis=0, keepdims=True)
    return jnp.concatenate([gain, bias, jnp.zeros((6, dh.shape[1]), F32)], axis=0)


def blocks_of(space):
    return ((0, PAD), (PAD, PAD)) if space else ((0, 192), (192, 200))


def keep_mask(space, size):
    row = lax.broadcasted_iota(jnp.int32, (size, size), 0)
    col = lax.broadcasted_iota(jnp.int32, (size, size), 1)
    if space:
        return col < PATCHES
    return (row >> 3) == (col >> 3)


def head_lanes(size):
    lane = lax.broadcasted_iota(jnp.int32, (size, 192), 1)
    return [(lane >= j * HD) & (lane < (j + 1) * HD) for j in range(3)]


def attn_fwd_kernel(torus, space, norm, n_pieces, *refs):
    where_ref, x_ref, norms_ref = refs[:3]
    pieces = refs[3 : 3 + n_pieces]
    y_ref, q_ref, k_ref, v_ref, o_ref, high_ref = refs[3 + n_pieces : 9 + n_pieces]
    w_qk, w_vo, h_ref, sems = refs[9 + n_pieces :]
    step = pl.program_id(0)
    r = group_at(step)

    @pl.when(step == 0)
    def _():
        start_loads(torus, where_ref, pieces, (w_qk, w_vo), sems)
        scaled, _ = normed(x_ref[...].astype(F32))
        h_ref[...] = (scaled * norms_ref[norm : norm + 1] + norms_ref[3 + norm : 4 + norm]).astype(BF16)

    wait_loads(r, (w_qk, w_vo), sems)
    hidden = h_ref[...]
    qk = dot_nn(hidden, w_qk[r])
    w_two = w_vo[r]
    q_ref[0] = qk[:, :192].astype(BF16)
    k_ref[0] = qk[:, 192:].astype(BF16)
    v_ref[0] = dot_nn(hidden, w_two[:, :192]).astype(BF16)
    tops = [None, None, None]
    for start, size in blocks_of(space):
        q = q_ref[0, pl.ds(start, size), :]
        k = k_ref[0, pl.ds(start, size), :]
        v = v_ref[0, pl.ds(start, size), :]
        keep = keep_mask(space, size)
        lanes = head_lanes(size)
        mixed = None
        for j in range(3):
            logits = dot_nt(jnp.where(lanes[j], q, jnp.zeros_like(q)), k) * SCALE
            logits = jnp.where(keep, logits, -1e30)
            peak = jnp.max(logits, axis=-1, keepdims=True)
            exponent = jnp.exp(logits - peak)
            total = jnp.sum(exponent, axis=-1, keepdims=True)
            weights = (exponent * (1.0 / total)).astype(BF16)
            part = dot_nn(weights, v)
            mixed = part if mixed is None else jnp.where(lanes[j], part, mixed)
            if space:
                row = lax.broadcasted_iota(jnp.int32, (size, 1), 0)
                peak = jnp.where(row < PATCHES, peak, -1e30)
            top = jnp.max(peak, axis=0, keepdims=True)
            tops[j] = top if tops[j] is None else jnp.maximum(tops[j], top)
        o_ref[0, pl.ds(start, size), :] = mixed.astype(BF16)
    row8 = lax.broadcasted_iota(jnp.int32, (8, 128), 0)
    high = jnp.full((8, 128), -1e30, F32)
    for j in range(3):
        high = jnp.where(row8 == j, jnp.broadcast_to(tops[j], (8, 128)), high)
    high_ref[0] = high
    term = dot_nt(o_ref[0], w_two[:, 192:])

    @pl.when(step == 0)
    def _():
        y_ref[...] = term

    @pl.when(step > 0)
    def _():
        y_ref[...] += term


def whole(shape):
    return pl.BlockSpec(shape, lambda i: (0,) * len(shape))


def per_group(shape):
    return pl.BlockSpec((1,) + shape, lambda i: (group_at(i),) + (0,) * len(shape))


def attn_fwd(torus, space, norm, where, x, norms, pieces):
    n, width = x.shape
    kernel = functools.partial(attn_fwd_kernel, torus, space, norm, len(pieces))
    heads = jax.ShapeDtypeStruct((4, n, 192), BF16)
    return pl.pallas_call(
        kernel,
        grid=(4,),
        out_shape=(
            jax.ShapeDtypeStruct((n, width), F32),
            heads,
            heads,
            heads,
            heads,
            jax.ShapeDtypeStruct((4, 8, 128), F32),
        ),
        in_specs=[pl.BlockSpec(memory_space=pltpu.SMEM), whole((n, width)), whole(norms.shape)]
        + [pl.BlockSpec(memory_space=pl.ANY)] * len(pieces),
        out_specs=(whole((n, width)),)
        + (per_group((n, 192)),) * 4
        + (per_group((8, 128)),),
        scratch_shapes=[
            pltpu.VMEM((4, width, 384), BF16),
            pltpu.VMEM((4, width, 384), BF16),
            pltpu.VMEM((n, width), BF16),
            pltpu.SemaphoreType.DMA((4, 2)),
        ],
        compiler_params=pltpu.CompilerParams(vmem_limit_bytes=VMEM_LIMIT),
        cost_estimate=pl.CostEstimate(flops=3 * 10**9, bytes_accessed=12 * 10**6, transcendentals=10**6),
        name="attn_fwd_space" if space else "attn_fwd_time",
    )(where, x, norms, *pieces)


def attn_bwd_kernel(torus, space, norm, n_pieces, rows, *refs):
    where_ref, dy_in, x_ref, norms_ref, q_ref, k_ref, v_ref, o_ref = refs[:8]
    refs = refs[8:]
    mixer = rows > 192
    if mixer:
        dmix_ref = refs[0]
        refs = refs[1:]
    pieces = refs[:n_pieces]
    dx_ref, sums_ref, g0_ref, g1_ref = refs[n_pieces : n_pieces + 4]
    w_qk, w_vo, h_ref, scaled_ref, dh_ref, dy_ref, dq_ref, dk_ref, dv_ref, sems = refs[n_pieces + 4 :]
    step = pl.program_id(0)
    r = group_at(step)

    @pl.when(step == 0)
    def _():
        start_loads(torus, where_ref, pieces, (w_qk, w_vo), sems)
        scaled, _ = normed(x_ref[...].astype(F32))
        scaled_ref[...] = scaled
        h_ref[...] = (scaled * norms_ref[norm : norm + 1] + norms_ref[3 + norm : 4 + norm]).astype(BF16)
        dy_ref[...] = dy_in[...].astype(BF16)
        dh_ref[...] = jnp.zeros_like(dh_ref)

    wait_loads(r, (w_qk, w_vo), sems)
    dy = dy_ref[...]
    w_two = w_vo[r]
    dmixed = dot_nn(dy, w_two)[:, 192:].astype(BF16)
    dv_ref[...] = dmixed
    for start, size in blocks_of(space):
        q = q_ref[0, pl.ds(start, size), :]
        k = k_ref[0, pl.ds(start, size), :]
        v = v_ref[0, pl.ds(start, size), :]
        do = dv_ref[pl.ds(start, size), :]
        keep = keep_mask(space, size)
        lanes = head_lanes(size)
        dq = dk = dv = None
        for j in range(3):
            zero = jnp.zeros_like(q)
            logits = dot_nt(jnp.where(lanes[j], q, zero), k) * SCALE
            logits = jnp.where(keep, logits, -1e30)
            peak = jnp.max(logits, axis=-1, keepdims=True)
            exponent = jnp.exp(logits - peak)
            total = jnp.sum(exponent, axis=-1, keepdims=True)
            weights = exponent * (1.0 / total)
            dweights = dot_nt(jnp.where(lanes[j], do, zero), v)
            inner = jnp.sum(dweights * weights, axis=-1, keepdims=True)
            dlogits = (weights * (dweights - inner)).astype(BF16)
            dv_j = dot_tn(weights.astype(BF16), do)
            dq_j = dot_nn(dlogits, k)
            dk_j = dot_tn(dlogits, q)
            dq = dq_j if dq is None else jnp.where(lanes[j], dq_j, dq)
            dk = dk_j if dk is None else jnp.where(lanes[j], dk_j, dk)
            dv = dv_j if dv is None else jnp.where(lanes[j], dv_j, dv)
        dq_ref[pl.ds(start, size), :] = (dq * SCALE).astype(BF16)
        dk_ref[pl.ds(start, size), :] = (dk * SCALE).astype(BF16)
        dv_ref[pl.ds(start, size), :] = dv.astype(BF16)
    hidden = h_ref[...]
    dqk = jnp.concatenate([dq_ref[...], dk_ref[...]], axis=1)
    dv = dv_ref[...]
    dh_ref[...] += dot_nt(dqk, w_qk[r]) + dot_nt(dv, w_two[:, :192])
    g_qk = dot_tn(hidden, dqk).astype(BF16)
    g_vo = jnp.concatenate([dot_tn(hidden, dv), dot_tn(dy, o_ref[0])], axis=1).astype(BF16)

    def put(g_ref):
        for dp in range(8):
            slot = out_slot(torus, where_ref, dp)
            g_ref[0, slot, 0:96, :] = g_qk[dp * 96 : (dp + 1) * 96]
            g_ref[0, slot, 96:192, :] = g_vo[dp * 96 : (dp + 1) * 96]
            if mixer:
                t = where_ref[2] ^ r
                block = dmix_ref[pl.ds(pl.multiple_of(dp * 96 + t * 24, 8), 24), :]
                g_ref[0, slot, 192:240, :] = jnp.concatenate([block[:, :384], block[:, 384:]], axis=0).astype(BF16)

    @pl.when(step < 2)
    def _():
        put(g1_ref)

    @pl.when(step >= 2)
    def _():
        put(g0_ref)

    @pl.when(step == 3)
    def _():
        _, inverse = normed(x_ref[...].astype(F32))
        scaled = scaled_ref[...]
        dh = dh_ref[...]
        dx_ref[...] = norm_back(dh, scaled, inverse, norms_ref[norm : norm + 1]).astype(dx_ref.dtype)
        sums_ref[...] = norm_sums(dh, scaled)


def grad_specs(rows, lanes):
    shape = (1, 8, rows, lanes)
    last = (0, 0, 0)
    return (
        pl.BlockSpec(shape, lambda i: (jnp.maximum(i - 2, 0),) + last),
        pl.BlockSpec(shape, lambda i: (jnp.minimum(i, 1),) + last),
    )


def attn_bwd(torus, space, norm, where, dy, x, norms, saved, pieces, dmix=None, out_type=F32):
    n, width = x.shape
    rows = 192 if dmix is None else 240
    kernel = functools.partial(attn_bwd_kernel, torus, space, norm, len(pieces), rows)
    extra = [] if dmix is None else [dmix]
    grads = jax.ShapeDtypeStruct((2, 8, rows, 384), BF16)
    return pl.pallas_call(
        kernel,
        grid=(4,),
        out_shape=(
            jax.ShapeDtypeStruct((n, width), out_type),
            jax.ShapeDtypeStruct((8, width), F32),
            grads,
            grads,
        ),
        in_specs=[
            pl.BlockSpec(memory_space=pltpu.SMEM),
            whole((n, width)),
            whole((n, width)),
            whole(norms.shape),
        ]
        + [per_group((n, 192))] * 4
        + [whole(e.shape) for e in extra]
        + [pl.BlockSpec(memory_space=pl.ANY)] * len(pieces),
        out_specs=(whole((n, width)), whole((8, width))) + grad_specs(rows, 384),
        scratch_shapes=[
            pltpu.VMEM((4, width, 384), BF16),
            pltpu.VMEM((4, width, 384), BF16),
            pltpu.VMEM((n, width), BF16),
            pltpu.VMEM((n, width), F32),
            pltpu.VMEM((n, width), F32),
            pltpu.VMEM((n, width), BF16),
            pltpu.VMEM((n, 192), BF16),
            pltpu.VMEM((n, 192), BF16),
            pltpu.VMEM((n, 192), BF16),
            pltpu.SemaphoreType.DMA((4, 2)),
        ],
        compiler_params=pltpu.CompilerParams(vmem_limit_bytes=VMEM_LIMIT),
        cost_estimate=pl.CostEstimate(flops=7 * 10**9, bytes_accessed=20 * 10**6, transcendentals=10**6),
        name="attn_bwd_space" if space else "attn_bwd_time",
    )(where, dy, x, norms, *saved, *extra, *pieces)


def hidden_kernel(torus, n_pieces, *refs):
    where_ref, x_ref, norms_ref, ct_ref = refs[:4]
    pieces = refs[4 : 4 + n_pieces]
    out_ref, dx_ref, sums_ref, g0_ref, g1_ref = refs[4 + n_pieces : 9 + n_pieces]
    w_in, w_out, h_ref, scaled_ref, dh_ref, sems = refs[9 + n_pieces :]
    step = pl.program_id(0)
    r = group_at(step)

    @pl.when(step == 0)
    def _():
        start_loads(torus, where_ref, pieces, (w_in, w_out), sems)
        x = x_ref[...]
        scaled, _ = normed(x)
        scaled_ref[...] = scaled
        h_ref[...] = (scaled * norms_ref[2:3] + norms_ref[5:6]).astype(BF16)
        dh_ref[...] = jnp.zeros_like(dh_ref)
        out_ref[...] = x

    wait_loads(r, (w_in, w_out), sems)
    hidden = h_ref[...]
    ct = ct_ref[...]
    up, down = w_in[r], w_out[r]
    pre = dot_nn(hidden, up)
    bell = 0.5 * (1.0 + lax.erf(pre * 0.7071067811865476))
    active = (pre * bell).astype(BF16)
    slope = bell + pre * (jnp.exp(-0.5 * pre * pre) * 0.3989422804014327)
    dpre = (dot_nn(ct, down) * slope).astype(BF16)
    out_ref[...] += dot_nt(active, down)
    dh_ref[...] += dot_nt(dpre, up)
    g_in = dot_tn(hidden, dpre).astype(BF16)
    g_out = dot_tn(ct, active).astype(BF16)

    def put(g_ref):
        for dp in range(8):
            slot = out_slot(torus, where_ref, dp)
            g_ref[0, slot, 0:96, :] = g_in[dp * 96 : (dp + 1) * 96]
            g_ref[0, slot, 96:192, :] = g_out[dp * 96 : (dp + 1) * 96]

    @pl.when(step < 2)
    def _():
        put(g1_ref)

    @pl.when(step >= 2)
    def _():
        put(g0_ref)

    @pl.when(step == 3)
    def _():
        _, inverse = normed(x_ref[...])
        scaled = scaled_ref[...]
        dh = dh_ref[...]
        dx_ref[...] = ct_ref[...].astype(F32) + norm_back(dh, scaled, inverse, norms_ref[2:3])
        sums_ref[...] = norm_sums(dh, scaled)


def hidden_both(torus, where, x, norms, ct, pieces):
    n, width = x.shape
    kernel = functools.partial(hidden_kernel, torus, len(pieces))
    grads = jax.ShapeDtypeStruct((2, 8, 192, 768), BF16)
    return pl.pallas_call(
        kernel,
        grid=(4,),
        out_shape=(
            jax.ShapeDtypeStruct((n, width), F32),
            jax.ShapeDtypeStruct((n, width), F32),
            jax.ShapeDtypeStruct((8, width), F32),
            grads,
            grads,
        ),
        in_specs=[
            pl.BlockSpec(memory_space=pltpu.SMEM),
            whole((n, width)),
            whole(norms.shape),
            whole((n, width)),
        ]
        + [pl.BlockSpec(memory_space=pl.ANY)] * len(pieces),
        out_specs=(whole((n, width)), whole((n, width)), whole((8, width))) + grad_specs(192, 768),
        scratch_shapes=[
            pltpu.VMEM((4, width, 768), BF16),
            pltpu.VMEM((4, width, 768), BF16),
            pltpu.VMEM((n, width), BF16),
            pltpu.VMEM((n, width), F32),
            pltpu.VMEM((n, width), F32),
            pltpu.SemaphoreType.DMA((4, 2)),
        ],
        compiler_params=pltpu.CompilerParams(vmem_limit_bytes=VMEM_LIMIT),
        cost_estimate=pl.CostEstimate(flops=12 * 10**9, bytes_accessed=25 * 10**6, transcendentals=3 * 10**6),
        name="hidden_both",
    )(where, x, norms, ct, *pieces)


def place_kernel(n_pieces, *refs):
    where_ref = refs[0]
    pieces = refs[1 : 1 + n_pieces]
    mixer_ref, norms_ref, held = refs[1 + n_pieces :]
    x = where_ref[1]
    zs = slot_rows(where_ref)
    left = jnp.zeros((8, 384), F32)
    right = jnp.zeros((8, 384), F32)
    for r in range(4):
        t = where_ref[2] ^ r
        for rx in range(2):
            for slot in range(4):
                which, lead = piece_of(r, rx, slot)
                row = pl.multiple_of((zs[slot] * 2 + (x ^ rx)) * 96 + t * 24, 8)
                tail = pieces[which][lead].astype(F32)
                held[pl.ds(row, 24), 0:384] = tail[0:24]
                held[pl.ds(row, 24), 384:768] = tail[24:48]
                left = left + tail[48:56]
                right = right + tail[56:64]
    norms_ref[...] = jnp.concatenate([left, right], axis=1)
    mixer_ref[...] = held[...].astype(BF16)


def place_mixer(where, pieces):
    return pl.pallas_call(
        functools.partial(place_kernel, len(pieces)),
        grid=(1,),
        out_shape=(jax.ShapeDtypeStruct((768, 768), BF16), jax.ShapeDtypeStruct((8, 768), F32)),
        in_specs=[pl.BlockSpec(memory_space=pltpu.SMEM)]
        + [pl.BlockSpec((p.shape[0], 64, 384), lambda i: (0, 3, 0)) for p in pieces],
        out_specs=(whole((768, 768)), whole((8, 768))),
        scratch_shapes=[pltpu.VMEM((768, 768), F32)],
        compiler_params=pltpu.CompilerParams(vmem_limit_bytes=VMEM_LIMIT),
        cost_estimate=pl.CostEstimate(flops=10**6, bytes_accessed=4 * 10**6, transcendentals=0),
        name="place_mixer",
    )(where, *pieces)


def gather_pieces(shard, inner):
    pair = jnp.stack([shard, send(shard, SWAP_Z1)])
    middle = send(pair, Z_MID)
    outer = send(middle, Z_OUT)
    own = jnp.concatenate([pair, jnp.where(inner, middle, outer)], axis=0)
    by_x = send(own, SWAP_X)
    by_y = send(own, SWAP_Y)
    both_a = send(by_x[:2], SWAP_Y)
    both_b = send(by_y[2:], SWAP_X)
    five = [own, by_x, by_y, both_a, both_b]
    return five + [send(v, SWAP_C) for v in five]


def plus(a, b):
    return (a.astype(F32) + b.astype(F32)).astype(BF16)


def reduce_pieces(g_keep, g_send, z):
    held = plus(g_keep, send(g_send, SWAP_C))
    own, by_x, by_y, both = held[0, :4], held[0, 4:], held[1, :4], held[1, 4:]
    got_a = send(both[:2], SWAP_Y)
    got_b = send(both[2:], SWAP_X)
    by_x = jnp.concatenate([plus(by_x[:2], got_a), by_x[2:]], axis=0)
    by_y = jnp.concatenate([by_y[:2], plus(by_y[2:], got_b)], axis=0)
    own = (
        own.astype(F32) + send(by_x, SWAP_X).astype(F32) + send(by_y, SWAP_Y).astype(F32)
    ).astype(BF16)
    near, far = own[:2], own[2:]
    far = plus(far, send(far, Z_IN))
    near = plus(near, send(far, Z_MID))
    low = (z & 1) == 0
    mine = jnp.where(low, near[0], near[1])
    other = jnp.where(low, near[1], near[0])
    return mine.astype(F32) + send(other, SWAP_Z1).astype(F32)


def pack_attn(w_qkv, w_out):
    top = jnp.concatenate([w_qkv[0], w_qkv[1]], axis=1)
    low = jnp.concatenate([w_qkv[2], w_out.T], axis=1)
    return jnp.stack([top, low])


def unpack_attn(piece):
    grad_qkv = jnp.stack([piece[0, :, :192], piece[0, :, 192:], piece[1, :, :192]])
    return grad_qkv, piece[1, :, 192:].T


def full_gather(packed):
    return lax.all_gather(lax.all_gather(packed, "dp", axis=1, tiled=True), "tensor", axis=0)


def full_reduce(g_keep, g_send):
    rows, lanes = g_keep.shape[2:]
    full = jnp.stack([g_keep[0], g_send[0], g_keep[1], g_send[1]]).reshape(4, 8, 2, rows // 2, lanes)
    full = full.transpose(0, 2, 1, 3, 4).reshape(4, 2, 4 * rows, lanes).astype(F32)
    mine = lax.psum_scatter(full, "tensor", scatter_dimension=0, tiled=False)
    return lax.psum_scatter(mine, "dp", scatter_dimension=1, tiled=True)


def exchange(torus, groups, t):
    if not torus:
        return lax.all_to_all(groups, "tensor", 0, 0, tiled=True)
    routes = (SWAP_C, SWAP_Y, SWAP_YC)
    got = [groups[0]] + [send(groups[i + 1], routes[i]) for i in range(3)]
    return jnp.stack(got)


def reorder(torus, groups, t):
    if not torus:
        return groups
    swap_c = (t & 1) == 1
    swap_y = (t >> 1) == 1
    groups = jnp.where(swap_c, jnp.stack([groups[1], groups[0], groups[3], groups[2]]), groups)
    return jnp.where(swap_y, jnp.stack([groups[2], groups[3], groups[0], groups[1]]), groups)


def to_patches(torus, rows, t):
    width = rows.shape[-1]
    groups = rows.reshape(2, 4, 49, width).transpose(1, 0, 2, 3)
    got = exchange(torus, reorder(torus, groups, t), t)
    return got.transpose(2, 0, 1, 3).reshape(392, width)


def to_frames(torus, rows, t):
    width = rows.shape[-1]
    groups = rows.reshape(49, 4, 2, width).transpose(1, 2, 0, 3)
    got = reorder(torus, exchange(torus, groups, t), t)
    return got.transpose(1, 0, 2, 3).reshape(2, PATCHES, width)


def padded(frames):
    return jnp.pad(frames, ((0, 0), (0, PAD - PATCHES), (0, 0))).reshape(2 * PAD, -1)


def trimmed(rows):
    return rows.reshape(2, PAD, -1)[:, :PATCHES]


def shards(
    torus,
    dp_size,
    clip_tokens,
    time_qkv,
    time_out,
    time_mixer,
    space_qkv,
    space_out,
    hidden_in,
    hidden_out,
    norm_gain,
    norm_bias,
    cotangent,
):
    dp = lax.axis_index("dp")
    t = lax.axis_index("tensor")
    z, x = dp >> 1, dp & 1
    where = jnp.stack([z, x, t, t]).astype(jnp.int32)
    width = clip_tokens.shape[-1]
    tokens = clip_tokens[0]
    ct = padded(cotangent[0].reshape(2, PATCHES, width))
    base = padded(tokens.reshape(2, PATCHES, width)).astype(F32)
    by_patch = to_patches(torus, tokens, t)

    time_w = pack_attn(time_qkv, time_out)
    space_w = pack_attn(space_qkv, space_out)
    ff_w = jnp.stack([hidden_in, hidden_out.T])
    norm_rows = jnp.concatenate([norm_gain, norm_bias], axis=0)
    share = norm_rows.shape[1]
    if torus:
        inner = (z == 1) | (z == 2)
        spread = lax.dynamic_update_slice(
            jnp.zeros((8, width), BF16), norm_rows, (0, (dp * 4 + t) * share)
        )
        time_shard = jnp.concatenate(
            [
                time_w.reshape(192, 384),
                time_mixer[:, :384],
                time_mixer[:, 384:],
                spread[:, :384],
                spread[:, 384:],
            ],
            axis=0,
        )
        time_p = gather_pieces(time_shard, inner)
        space_p = gather_pieces(space_w.reshape(192, 384), inner)
        ff_p = gather_pieces(ff_w.reshape(192, 768), inner)
        mixer, norms = place_mixer(where, time_p)
    else:
        time_p = [full_gather(time_w)]
        space_p = [full_gather(space_w)]
        ff_p = [full_gather(ff_w)]
        mixer = lax.all_gather(time_mixer, AXES, axis=0, tiled=True)
        norms = lax.all_gather(norm_rows, AXES, axis=1, tiled=True).astype(F32)
        norms = jnp.pad(norms, ((0, 2), (0, 0)))

    y_time, *kept_time, high_time = attn_fwd(torus, False, 0, where, by_patch, norms, time_p)
    mixer_in = padded(to_frames(torus, y_time.astype(BF16), t))
    after_time = base + jnp.dot(mixer_in, mixer, preferred_element_type=F32)
    y_space, *kept_space, high_space = attn_fwd(torus, True, 1, where, after_time, norms, space_p)
    after_space = after_time + y_space
    out_rows, d_space, sums_three, g0_ff, g1_ff = hidden_both(
        torus, where, after_space, norms, ct, ff_p
    )
    dln_two, sums_two, g0_space, g1_space = attn_bwd(
        torus, True, 1, where, d_space, after_time, norms, kept_space, space_p
    )
    d_time = d_space + dln_two
    d_time_low = d_time.astype(BF16)
    dmix = lax.dot_general(
        mixer_in, d_time_low, (((0,), (0,)), ((), ())), preferred_element_type=F32
    )
    d_mixer_in = lax.dot_general(
        d_time_low, mixer, (((1,), (1,)), ((), ())), preferred_element_type=F32
    ).astype(BF16)
    d_patch = to_patches(torus, trimmed(d_mixer_in).reshape(392, width), t)
    dln_one, sums_one, g0_time, g1_time = attn_bwd(
        torus,
        False,
        0,
        where,
        d_patch,
        by_patch,
        norms,
        kept_time,
        time_p,
        dmix=dmix if torus else None,
        out_type=BF16,
    )
    back = to_frames(torus, dln_one, t).astype(F32)
    input_grad = trimmed(d_time) + back

    highs = jnp.stack([high_time[:, :3, 0], high_space[:, :3, 0]], axis=1)
    sums = jnp.concatenate(
        [sums_one[:1], sums_two[:1], sums_three[:1], sums_one[1:2], sums_two[1:2], sums_three[1:2]]
    )
    if torus:
        ff = reduce_pieces(g0_ff, g1_ff, z).reshape(2, 96, 768)
        space = reduce_pieces(g0_space, g1_space, z).reshape(2, 96, 384)
        timed = reduce_pieces(g0_time, g1_time, z)
        mixer_grad = jnp.concatenate([timed[192:216], timed[216:240]], axis=1)
        timed = timed[:192].reshape(2, 96, 384)
        for route, flip in ((SWAP_C, 1), (SWAP_Y, 2), (SWAP_X, 0), (SWAP_Z1, 0), (SWAP_Z2, 0)):
            other = send(highs, route)
            highs = jnp.maximum(highs, jnp.stack([other[i ^ flip] for i in range(4)]))
            sums = sums + send(sums, route)
        highest = highs[0]
        mine = lax.dynamic_slice(sums, (0, (dp * 4 + t) * share), (6, share))
    else:
        ff = full_reduce(g0_ff, g1_ff)
        space = full_reduce(g0_space, g1_space)
        timed = full_reduce(g0_time, g1_time)
        mixer_grad = lax.psum_scatter(dmix, AXES, scatter_dimension=0, tiled=True)
        highest = lax.dynamic_index_in_dim(lax.pmax(highs, AXES), t, 0, keepdims=False)
        mine = lax.psum_scatter(sums, AXES, scatter_dimension=1, tiled=True)
    qk_clip = jnp.sqrt(TAU / jnp.maximum(highest, TAU))
    time_qkv_grad, time_out_grad = unpack_attn(timed)
    space_qkv_grad, space_out_grad = unpack_attn(space)
    return (
        trimmed(out_rows).reshape(1, 392, width),
        input_grad.reshape(1, 392, width),
        time_qkv_grad,
        time_out_grad,
        mixer_grad,
        space_qkv_grad,
        space_out_grad,
        ff[0],
        ff[1].T,
        mine[:3],
        mine[3:],
        qk_clip,
    )


def solution(mesh):
    sizes = dict(mesh.shape)
    torus = sizes["dp"] == 8 and sizes["tensor"] == 4
    in_specs = (
        P("dp", "tensor", None),
        P(None, "dp", "tensor"),
        P("tensor", "dp"),
        P(("dp", "tensor"), None),
        P(None, "dp", "tensor"),
        P("tensor", "dp"),
        P("dp", "tensor"),
        P("tensor", "dp"),
        P(None, ("dp", "tensor")),
        P(None, ("dp", "tensor")),
        P("dp", "tensor", None),
    )
    out_specs = (
        P("dp", "tensor", None),
        P("dp", "tensor", None),
        P(None, "dp", "tensor"),
        P("tensor", "dp"),
        P(("dp", "tensor"), None),
        P(None, "dp", "tensor"),
        P("tensor", "dp"),
        P("dp", "tensor"),
        P("tensor", "dp"),
        P(None, ("dp", "tensor")),
        P(None, ("dp", "tensor")),
        P(None, "tensor"),
    )
    body = functools.partial(shards, torus, sizes["dp"])
    return jax.shard_map(body, mesh=mesh, in_specs=in_specs, out_specs=out_specs, check_vma=False)
```

time: 1220 us -> 422 us (0.35)
  waiting for transfers between devices: 659 us -> 137 us
  blocking collectives: 283 us -> 0 us
  matrix products: 121 us -> 4.61 us
  Pallas kernels: 0 us -> 108 us
  starting transfers between devices: 2.13 us -> 88.8 us
  local copies, waits for them, and re-layouts: 105 us -> 36.7 us
  between operations: 17.1 us -> 2.06 us
    reduce_scatter x9 -> x0, waiting for transfers between devices: 393 us -> none  [the longest x1 104 us: shards(): lax.psum_scatter(grad_mixer, ('dp', 'tensor'), scatter_dimension=0, tiled...]
    all_gather x6 -> x0, blocking collectives: 222 us -> none  [the longest x2 77.7 us: fetch_attn(): lax.all_gather(weight_qkv, 'dp', axis=1, tiled=True)]
    unnamed x26 -> x0, waiting for transfers between devices: 154 us -> none
    ppermute x0 -> x82, waiting for transfers between devices: none -> 137 us  [send(): return lax.ppermute(value, AXES, route)]
    all_gather x9 -> x0, waiting for transfers between devices: 111 us -> none  [the longest x3 53.9 us: gather_grads(): return lax.all_gather(local_grad, 'tensor', axis=1, tiled=True)]
    pallas_call x0 -> x6, Pallas kernels: none -> 108 us  [the longest x2 53.7 us: attn_bwd(): pl.pallas_call(kernel, grid=(4,), out_shape=(jax.ShapeDtypeStruct((n, wid...]
    dot_general x29 -> x3, matrix products: 107 us -> 4.61 us  [the longest x1 2.21 us: shards(): lax.dot_general(mixer_in, d_time_low, (((0,), (0,)), ((), ())), preferred...]
    ppermute x0 -> x82, starting transfers between devices: none -> 88.8 us  [send(): return lax.ppermute(value, AXES, route)]
  transfers between devices with their start and end apart: 22 -> 82, of which waited for: 18 -> 38; matrix products, arithmetic and copies ran while one was open for 13% -> 17% of each run, Pallas kernels for 0% -> 14%
where the time goes in v1:
time: 422 us; the launch traced here: 416 us
  waiting for transfers between devices  137 us (32%)
  Pallas kernels  108 us (26%)
  starting transfers between devices  88.8 us (21%)
  other arithmetic  38.2 us (9%)
  local copies, waits for them, and re-layouts  36.7 us (9%)
  matrix products  4.61 us (1%)
    ppermute x82, waiting for transfers between devices, send(): return lax.ppermute(value, AXES, route)  137 us
    ppermute x82, starting transfers between devices, send(): return lax.ppermute(value, AXES, route)  88.8 us
    pallas_call x2, Pallas kernels, attn_bwd(): pl.pallas_call(kernel, grid=(4,), out_shape=(jax.ShapeDtypeStruct((n, wid...  53.7 us
    pallas_call x2, Pallas kernels, attn_fwd(): pl.pallas_call(kernel, grid=(4,), out_shape=(jax.ShapeDtypeStruct((n, wid...  29.7 us
    pallas_call x1, Pallas kernels, hidden_both(): pl.pallas_call(kernel, grid=(4,), out_shape=(jax.ShapeDtypeStruct((n, wid...  22.2 us
    convert_element_type x12, other arithmetic, plus(): return (a.astype(F32) + b.astype(F32)).astype(BF16)  14.5 us
  transfers between devices with their start and end apart: 82, of which 38 were waited for; matrix products, arithmetic and copies ran while one was open for 17% of the time, Pallas kernels for 14%

profile of v1, /device:TPU:0, one launch (start us, length us, event | category | flops | bytes accessed | tf_op | source)
XLA Modules:
  0.0 415.7 jit_solution(8564119540796357994)
XLA Ops:
  16.5 4.8 %collective-permute-done.30 = bf16[192,768]{1,0:T(8,128)(2,1)S(1)} collective-permute-done((bf16[192,768]{1,0:T(8,128)(2,1)S(1)}, bf16[192,768]{1,0:T(8,128)(2,1)S(1)}, u32[]{:S(2)}, u32[]{:S(2)}) %collective-permute-start.30) | collective-permute-done | bytes 294944 | tf_op jit(solution)/shard_map/ppermute | solution.py:46
  22.0 11.1 %collective-permute-done.5 = bf16[2,256,384]{2,1,0:T(8,128)(2,1)S(1)} collective-permute-done((bf16[2,256,384]{2,1,0:T(8,128)(2,1)S(1)}, bf16[2,256,384]{2,1,0:T(8,128)(2,1)S(1)}, u32[]{:S(2)}, u32[]{:S(2)}) %collective-permute-start.5) | collective-permute-done | bytes 393248 | tf_op jit(solution)/shard_map/ppermute | solution.py:46
  39.5 5.2 %collective-permute-done.20 = bf16[2,192,384]{2,1,0:T(8,128)(2,1)S(1)} collective-permute-done((bf16[2,192,384]{2,1,0:T(8,128)(2,1)S(1)}, bf16[2,192,384]{2,1,0:T(8,128)(2,1)S(1)}, u32[]{:S(2)}, u32[]{:S(2)}) %collective-permute-start.20) | collective-permute-done | bytes 294944 | tf_op jit(solution)/shard_map/ppermute | solution.py:46
  47.4 6.0 %collective-permute-done.2 = bf16[2,49,768]{2,1,0:T(8,128)(2,1)S(1)} collective-permute-done((bf16[2,49,768]{2,1,0:T(8,128)(2,1)S(1)}, bf16[2,49,768]{2,1,0:T(8,128)(2,1)S(1)}, u32[]{:S(2)}, u32[]{:S(2)}) %collective-permute-start.2) | collective-permute-done | bytes 150560 | tf_op jit(solution)/shard_map/ppermute | solution.py:46
  61.9 11.1 %collective-permute-done.22.refs_5_.refs_10_ = bf16[4,192,384]{2,1,0:T(8,128)(2,1)} collective-permute-done((bf16[4,192,384]{2,1,0:T(8,128)(2,1)}, bf16[4,192,384]{2,1,0:T(8,128)(2,1)}, u32[]{:S(2)}, u32[]{:S(2)}) %collective-permute-start.22) | collective-permute-done | bytes 589856 | tf_op jit(solution)/shard_map/ppermute | solution.py:46
  74.4 6.2 %collective-permute-done.9.refs_5_.refs_7_.refs_13_ = bf16[2,256,384]{2,1,0:T(8,128)(2,1)S(1)} collective-permute-done((bf16[2,256,384]{2,1,0:T(8,128)(2,1)S(1)}, bf16[2,256,384]{2,1,0:T(8,128)(2,1)S(1)}, u32[]{:S(2)}, u32[]{:S(2)}) %collective-permute-start.9) | collective-permute-done | bytes 393248 | tf_op jit(solution)/shard_map/ppermute | solution.py:46
  95.7 15.2 %attn_fwd_time.1 = (f32[392,768]{1,0:T(8,128)}, bf16[4,392,192]{2,1,0:T(8,128)(2,1)}, bf16[4,392,192]{2,1,0:T(8,128)(2,1)}, bf16[4,392,192]{2,1,0:T(8,128)(2,1)}...) custom-call(s32[4]{0:T(128)} %pad_add_fusion.refs_0_, bf16[392,768]{1,0:T(8,128)(2,1)} %reshape.145.refs_1_.refs_2_, ...), custom_call_target="tpu_custom_call" | custom-call | flops 3000000000 | bytes 12000000 | tf_op jit(solution)/shard_map/attn_fwd_time/pallas_call | solution.py:226
  131.4 14.5 %attn_fwd_space.1 = (f32[416,768]{1,0:T(8,128)}, bf16[4,416,192]{2,1,0:T(8,128)(2,1)}, bf16[4,416,192]{2,1,0:T(8,128)(2,1)}, bf16[4,416,192]{2,1,0:T(8,128)(2,1)...) custom-call(s32[4]{0:T(128)} %pad_add_fusion.refs_0_, f32[416,768]{1,0:T(8,128)} %convolution_add_fusion.refs_1_.refs_2_, ...), custom_call_target="tpu_custom_call" | custom-call | flops 3000000000 | bytes 12000000 | tf_op jit(solution)/shard_map/attn_fwd_space/pallas_call | solution.py:226
  155.4 22.2 %hidden_both.1 = (f32[416,768]{1,0:T(8,128)}, f32[416,768]{1,0:T(8,128)}, f32[8,768]{1,0:T(8,128)}, bf16[2,8,192,768]{3,2,1,0:T(8,128)(2,1)}, bf16[2,8,192,768]{3,2,1,0:T(8,128)(2,1)}) custom-call(s32[4]{0:T(128)} %pad_add_fusion.refs_0_, f32[416,768]{1,0:T(8,128)} %add.116.refs_1_, f32[8,768]{1,0:T(8,128)} %get-tuple-element.39.refs_2_.refs_3_, ...), custom_call_target="tpu_custom_call" | custom-call | flops 12000000000 | bytes 25000000 | tf_op jit(solution)/shard_map/hidden_both/pallas_call | solution.py:454
  177.7 27.1 %attn_bwd_space.1 = (f32[416,768]{1,0:T(8,128)}, f32[8,768]{1,0:T(8,128)}, bf16[2,8,192,384]{3,2,1,0:T(8,128)(2,1)}, bf16[2,8,192,384]{3,2,1,0:T(8,128)(2,1)}) custom-call(s32[4]{0:T(128)} %pad_add_fusion.refs_0_, f32[416,768]{1,0:T(8,128)} %get-tuple-element.44.refs_1_, f32[416,768]{1,0:T(8,128)} %convolution_add_fusion.refs_1_.refs_2_, ...), custom_call_target="tpu_custom_call" | custom-call | flops 7000000000 | bytes 20000000 | tf_op jit(solution)/shard_map/attn_bwd_space/pallas_call | solution.py:358
  215.4 3.9 collective-permute-done.43
  221.0 26.6 %attn_bwd_time.1 = (bf16[392,768]{1,0:T(8,128)(2,1)}, f32[8,768]{1,0:T(8,128)}, bf16[2,8,240,384]{3,2,1,0:T(8,128)(2,1)}, bf16[2,8,240,384]{3,2,1,0:T(8,128)(2,1)}) custom-call(s32[4]{0:T(128)} %pad_add_fusion.refs_0_, bf16[392,768]{1,0:T(8,128)(2,1)} %reshape.157.refs_1_, bf16[392,768]{1,0:T(8,128)(2,1)} %reshape.145.refs_1_.refs_2_, ...), custom_call_target="tpu_custom_call" | custom-call | flops 7000000000 | bytes 20000000 | tf_op jit(solution)/shard_map/attn_bwd_time/pallas_call | solution.py:358
  277.7 6.4 %collective-permute-done.57 = bf16[2,192,384]{2,1,0:T(8,128)(2,1)S(1)} collective-permute-done((bf16[2,192,384]{2,1,0:T(8,128)(2,1)S(1)}, bf16[2,192,384]{2,1,0:T(8,128)(2,1)S(1)}, u32[]{:S(2)}, u32[]{:S(2)}) %collective-permute-start.57) | collective-permute-done | bytes 294944 | tf_op jit(solution)/shard_map/ppermute | solution.py:46
  286.5 4.2 %collective-permute-done.47 = bf16[2,49,768]{2,1,0:T(8,128)(2,1)S(1)} collective-permute-done((bf16[2,49,768]{2,1,0:T(8,128)(2,1)S(1)}, bf16[2,49,768]{2,1,0:T(8,128)(2,1)S(1)}, u32[]{:S(2)}, u32[]{:S(2)}) %collective-permute-start.47) | collective-permute-done | bytes 150560 | tf_op jit(solution)/shard_map/ppermute | solution.py:46
  295.0 10.8 %collective-permute-done.60 = bf16[4,192,384]{2,1,0:T(8,128)(2,1)S(1)} collective-permute-done((bf16[4,192,384]{2,1,0:T(8,128)(2,1)S(1)}, bf16[4,192,384]{2,1,0:T(8,128)(2,1)S(1)}, u32[]{:S(2)}, u32[]{:S(2)}) %collective-permute-start.60) | collective-permute-done | bytes 589856 | tf_op jit(solution)/shard_map/ppermute | solution.py:46
  306.1 3.9 collective-permute-start.61
  316.8 3.8 add_convert_fusion
  326.4 10.7 %collective-permute-done.65 = bf16[2,192,768]{2,1,0:T(8,128)(2,1)S(1)} collective-permute-done((bf16[2,192,768]{2,1,0:T(8,128)(2,1)S(1)}, bf16[2,192,768]{2,1,0:T(8,128)(2,1)S(1)}, u32[]{:S(2)}, u32[]{:S(2)}) %collective-permute-start.65) | collective-permute-done | bytes 589856 | tf_op jit(solution)/shard_map/ppermute | solution.py:46
  346.4 6.4 %collective-permute-done.52 = bf16[4,240,384]{2,1,0:T(8,128)(2,1)S(1)} collective-permute-done((bf16[4,240,384]{2,1,0:T(8,128)(2,1)S(1)}, bf16[4,240,384]{2,1,0:T(8,128)(2,1)S(1)}, u32[]{:S(2)}, u32[]{:S(2)}) %collective-permute-start.52) | collective-permute-done | bytes 737312 | tf_op jit(solution)/shard_map/ppermute | solution.py:46
  354.8 5.7 %collective-permute-start.53 = (bf16[2,240,384]{2,1,0:T(8,128)(2,1)}, bf16[2,240,384]{2,1,0:T(8,128)(2,1)}, u32[]{:S(2)}, u32[]{:S(2)}) collective-permute-start(bf16[2,240,384]{2,1,0:T(8,128)(2,1)} %slice.631), channel_id=1, source_target_pairs={{0,8},{1,9},{2,10},{3,11},{4,12},{5,13},{6,14},{7,15},{24,16},{25,... | collective-permute-start | bytes 1105928 | tf_op jit(solution)/shard_map/ppermute | solution.py:46
  368.3 7.6 %collective-permute-done.68 = bf16[4,192,768]{2,1,0:T(8,128)(2,1)} collective-permute-done((bf16[4,192,768]{2,1,0:T(8,128)(2,1)}, bf16[4,192,768]{2,1,0:T(8,128)(2,1)}, u32[]{:S(2)}, u32[]{:S(2)}) %collective-permute-start.68) | collective-permute-done | bytes 1179680 | tf_op jit(solution)/shard_map/ppermute | solution.py:46
  379.8 3.9 collective-permute-start.69
  385.8 9.5 %collective-permute-done.69 = bf16[2,192,768]{2,1,0:T(8,128)(2,1)S(1)} collective-permute-done((bf16[2,192,768]{2,1,0:T(8,128)(2,1)}, bf16[2,192,768]{2,1,0:T(8,128)(2,1)S(1)}, u32[]{:S(2)}, u32[]{:S(2)}) %collective-permute-start.69) | collective-permute-done | bytes 589856 | tf_op jit(solution)/shard_map/ppermute | solution.py:46
  397.5 12.3 %collective-permute-start.71 = (bf16[192,768]{1,0:T(8,128)(2,1)S(1)}, bf16[192,768]{1,0:T(8,128)(2,1)S(1)}, u32[]{:S(2)}, u32[]{:S(2)}) collective-permute-start(bf16[192,768]{1,0:T(8,128)(2,1)S(1)} %select_bitcast_fusion), channel_id=1, source_target_pairs={{0,8},{1,9},{2,10},{3,11},{4,12},{5,13},{6,14},{7,15},{8,0},{9,1},... | collective-permute-start | bytes 884744 | tf_op jit(solution)/shard_map/ppermute | solution.py:46
  (363 shorter events, 174.5 us)
Async XLA Ops:
  13.5 19.5 %collective-permute-start.5 = (bf16[2,256,384]{2,1,0:T(8,128)(2,1)S(1)}, bf16[2,256,384]{2,1,0:T(8,128)(2,1)S(1)}, u32[]{:S(2)}, u32[]{:S(2)}) collective-permute-start(bf16[2,256,384]{2,1,0:T(8,128)(2,1)S(1)} %collective-permute-done.4), channel_id=1, source_target_pairs={{8,0},{9,1},{10,2},{11,3},{12,4},{13,5},{14,6},{15,7},{16,24},{17,... | collective-permute-start | bytes 1179656 | tf_op jit(solution)/shard_map/ppermute | solution.py:46
  15.8 19.1 %collective-permute-start.19 = (bf16[2,192,384]{2,1,0:T(8,128)(2,1)S(1)}, bf16[2,192,384]{2,1,0:T(8,128)(2,1)S(1)}, u32[]{:S(2)}, u32[]{:S(2)}) collective-permute-start(bf16[2,192,384]{2,1,0:T(8,128)(2,1)S(1)} %pad_maximum_fusion.11), channel_id=1, source_target_pairs={{8,16},{9,17},{10,18},{11,19},{12,20},{13,21},{14,22},{15,23},{16,... | collective-permute-start | bytes 884744 | tf_op jit(solution)/shard_map/ppermute | solution.py:46
  21.3 24.8 %collective-permute-start.31 = (bf16[2,192,768]{2,1,0:T(8,128)(2,1)S(1)}, bf16[2,192,768]{2,1,0:T(8,128)(2,1)S(1)}, u32[]{:S(2)}, u32[]{:S(2)}) collective-permute-start(bf16[2,192,768]{2,1,0:T(8,128)(2,1)S(1)} %pad_maximum_fusion.7), channel_id=1, source_target_pairs={{8,16},{9,17},{10,18},{11,19},{12,20},{13,21},{14,22},{15,23},{16,... | collective-permute-start | bytes 1769480 | tf_op jit(solution)/shard_map/ppermute | solution.py:46
  33.2 24.5 %collective-permute-start.7 = (bf16[4,256,384]{2,1,0:T(8,128)(2,1)S(1)}, bf16[4,256,384]{2,1,0:T(8,128)(2,1)S(1)}, u32[]{:S(2)}, u32[]{:S(2)}) collective-permute-start(bf16[4,256,384]{2,1,0:T(8,128)(2,1)S(1)} %pad_maximum_fusion.3.refs_1_.refs_3_.refs_9_), channel_id=1, source_target_pairs={{0,2},{1,3},{2,0},{3,1},{4,6},{5,7},{6,4},{7,5},{8,10},{9,11},{10,... | collective-permute-start | bytes 2359304 | tf_op jit(solution)/shard_map/ppermute | solution.py:46
  36.1 23.2 %collective-permute-start.6 = (bf16[4,256,384]{2,1,0:T(8,128)(2,1)S(1)}, bf16[4,256,384]{2,1,0:T(8,128)(2,1)}, u32[]{:S(2)}, u32[]{:S(2)}) collective-permute-start(bf16[4,256,384]{2,1,0:T(8,128)(2,1)S(1)} %pad_maximum_fusion.3.refs_1_.refs_3_.refs_9_), channel_id=1, source_target_pairs={{0,4},{1,5},{2,6},{3,7},{4,0},{5,1},{6,2},{7,3},{8,12},{9,13},{10,... | collective-permute-start | bytes 2359304 | tf_op jit(solution)/shard_map/ppermute | solution.py:46
  53.4 28.3 %collective-permute-start.10 = (bf16[4,256,384]{2,1,0:T(8,128)(2,1)S(1)}, bf16[4,256,384]{2,1,0:T(8,128)(2,1)S(1)}, u32[]{:S(2)}, u32[]{:S(2)}) collective-permute-start(bf16[4,256,384]{2,1,0:T(8,128)(2,1)S(1)} %pad_maximum_fusion.3.refs_1_.refs_3_.refs_9_), channel_id=1, source_target_pairs={{0,1},{1,0},{2,3},{3,2},{4,5},{5,4},{6,7},{7,6},{8,9},{9,8},{10,11... | collective-permute-start | bytes 2359304 | tf_op jit(solution)/shard_map/ppermute | solution.py:46
  59.3 21.2 %collective-permute-start.9 = (bf16[2,256,384]{2,1,0:T(8,128)(2,1)S(1)}, bf16[2,256,384]{2,1,0:T(8,128)(2,1)S(1)}, u32[]{:S(2)}, u32[]{:S(2)}) collective-permute-start(bf16[2,256,384]{2,1,0:T(8,128)(2,1)S(1)} %slice.593), channel_id=1, source_target_pairs={{0,4},{1,5},{2,6},{3,7},{4,0},{5,1},{6,2},{7,3},{8,12},{9,13},{10,... | collective-permute-start | bytes 1179656 | tf_op jit(solution)/shard_map/ppermute | solution.py:46
  61.0 22.5 %collective-permute-start.8 = (bf16[2,256,384]{2,1,0:T(8,128)(2,1)S(1)}, bf16[2,256,384]{2,1,0:T(8,128)(2,1)}, u32[]{:S(2)}, u32[]{:S(2)}) collective-permute-start(bf16[2,256,384]{2,1,0:T(8,128)(2,1)S(1)} %slice.592), channel_id=1, source_target_pairs={{0,2},{1,3},{2,0},{3,1},{4,6},{5,7},{6,4},{7,5},{8,10},{9,11},{10,... | collective-permute-start | bytes 1179656 | tf_op jit(solution)/shard_map/ppermute | solution.py:46
  74.4 18.6 %collective-permute-start.11 = (bf16[4,256,384]{2,1,0:T(8,128)(2,1)}, bf16[4,256,384]{2,1,0:T(8,128)(2,1)}, u32[]{:S(2)}, u32[]{:S(2)}) collective-permute-start(bf16[4,256,384]{2,1,0:T(8,128)(2,1)} %collective-permute-done.6.refs_2_.refs_4_.refs_10_), channel_id=1, source_target_pairs={{0,1},{1,0},{2,3},{3,2},{4,5},{5,4},{6,7},{7,6},{8,9},{9,8},{10,11... | collective-permute-start | bytes 2359304 | tf_op jit(solution)/shard_map/ppermute | solution.py:46
  82.6 30.1 %collective-permute-start.34 = (bf16[4,192,768]{2,1,0:T(8,128)(2,1)}, bf16[4,192,768]{2,1,0:T(8,128)(2,1)}, u32[]{:S(2)}, u32[]{:S(2)}) collective-permute-start(bf16[4,192,768]{2,1,0:T(8,128)(2,1)} %pad_maximum_fusion.refs_4_), channel_id=1, source_target_pairs={{0,2},{1,3},{2,0},{3,1},{4,6},{5,7},{6,4},{7,5},{8,10},{9,11},{10,... | collective-permute-start | bytes 3538952 | tf_op jit(solution)/shard_map/ppermute | solution.py:46
  83.5 30.2 %collective-permute-start.33 = (bf16[4,192,768]{2,1,0:T(8,128)(2,1)}, bf16[4,192,768]{2,1,0:T(8,128)(2,1)}, u32[]{:S(2)}, u32[]{:S(2)}) collective-permute-start(bf16[4,192,768]{2,1,0:T(8,128)(2,1)} %pad_maximum_fusion.refs_4_), channel_id=1, source_target_pairs={{0,4},{1,5},{2,6},{3,7},{4,0},{5,1},{6,2},{7,3},{8,12},{9,13},{10,... | collective-permute-start | bytes 3538952 | tf_op jit(solution)/shard_map/ppermute | solution.py:46
  91.2 27.7 %collective-permute-start.24 = (bf16[2,192,384]{2,1,0:T(8,128)(2,1)}, bf16[2,192,384]{2,1,0:T(8,128)(2,1)}, u32[]{:S(2)}, u32[]{:S(2)}) collective-permute-start(bf16[2,192,384]{2,1,0:T(8,128)(2,1)} %slice.601), channel_id=1, source_target_pairs={{0,4},{1,5},{2,6},{3,7},{4,0},{5,1},{6,2},{7,3},{8,12},{9,13},{10,... | collective-permute-start | bytes 884744 | tf_op jit(solution)/shard_map/ppermute | solution.py:46
  91.8 27.5 %collective-permute-start.23 = (bf16[2,192,384]{2,1,0:T(8,128)(2,1)S(1)}, bf16[2,192,384]{2,1,0:T(8,128)(2,1)}, u32[]{:S(2)}, u32[]{:S(2)}) collective-permute-start(bf16[2,192,384]{2,1,0:T(8,128)(2,1)S(1)} %slice.600), channel_id=1, source_target_pairs={{0,2},{1,3},{2,0},{3,1},{4,6},{5,7},{6,4},{7,5},{8,10},{9,11},{10,... | collective-permute-start | bytes 884744 | tf_op jit(solution)/shard_map/ppermute | solution.py:46
  128.7 26.7 %collective-permute-start.37 = (bf16[4,192,768]{2,1,0:T(8,128)(2,1)}, bf16[4,192,768]{2,1,0:T(8,128)(2,1)}, u32[]{:S(2)}, u32[]{:S(2)}) collective-permute-start(bf16[4,192,768]{2,1,0:T(8,128)(2,1)} %pad_maximum_fusion.refs_4_), channel_id=1, source_target_pairs={{0,1},{1,0},{2,3},{3,2},{4,5},{5,4},{6,7},{7,6},{8,9},{9,8},{10,11... | collective-permute-start | bytes 3538952 | tf_op jit(solution)/shard_map/ppermute | solution.py:46
  129.0 19.3 %collective-permute-start.36 = (bf16[2,192,768]{2,1,0:T(8,128)(2,1)}, bf16[2,192,768]{2,1,0:T(8,128)(2,1)}, u32[]{:S(2)}, u32[]{:S(2)}) collective-permute-start(bf16[2,192,768]{2,1,0:T(8,128)(2,1)} %slice.603), channel_id=1, source_target_pairs={{0,4},{1,5},{2,6},{3,7},{4,0},{5,1},{6,2},{7,3},{8,12},{9,13},{10,... | collective-permute-start | bytes 1769480 | tf_op jit(solution)/shard_map/ppermute | solution.py:46
  210.8 61.7 %collective-permute-start.56 = (bf16[2,8,192,384]{3,2,1,0:T(8,128)(2,1)}, bf16[2,8,192,384]{3,2,1,0:T(8,128)(2,1)}, u32[]{:S(2)}, u32[]{:S(2)}) collective-permute-start(bf16[2,8,192,384]{3,2,1,0:T(8,128)(2,1)} %get-tuple-element.58), channel_id=1, source_target_pairs={{0,1},{1,0},{2,3},{3,2},{4,5},{5,4},{6,7},{7,6},{8,9},{9,8},{10,11... | collective-permute-start | bytes 7077896 | tf_op jit(solution)/shard_map/ppermute | solution.py:46
  210.8 105.9 %collective-permute-start.64 = (bf16[2,8,192,768]{3,2,1,0:T(8,128)(2,1)}, bf16[2,8,192,768]{3,2,1,0:T(8,128)(2,1)}, u32[]{:S(2)}, u32[]{:S(2)}) collective-permute-start(bf16[2,8,192,768]{3,2,1,0:T(8,128)(2,1)} %get-tuple-element.60), channel_id=1, source_target_pairs={{0,1},{1,0},{2,3},{3,2},{4,5},{5,4},{6,7},{7,6},{8,9},{9,8},{10,11... | collective-permute-start | bytes 14155784 | tf_op jit(solution)/shard_map/ppermute | solution.py:46
  249.8 60.3 %collective-permute-start.48 = (bf16[2,8,240,384]{3,2,1,0:T(8,128)(2,1)}, bf16[2,8,240,384]{3,2,1,0:T(8,128)(2,1)}, u32[]{:S(2)}, u32[]{:S(2)}) collective-permute-start(bf16[2,8,240,384]{3,2,1,0:T(8,128)(2,1)} %get-tuple-element.56), channel_id=1, source_target_pairs={{0,1},{1,0},{2,3},{3,2},{4,5},{5,4},{6,7},{7,6},{8,9},{9,8},{10,11... | collective-permute-start | bytes 8847368 | tf_op jit(solution)/shard_map/ppermute | solution.py:46
  285.7 20.2 %collective-permute-start.60 = (bf16[4,192,384]{2,1,0:T(8,128)(2,1)S(1)}, bf16[4,192,384]{2,1,0:T(8,128)(2,1)S(1)}, u32[]{:S(2)}, u32[]{:S(2)}) collective-permute-start(bf16[4,192,384]{2,1,0:T(8,128)(2,1)S(1)} %pad_maximum_fusion.9), channel_id=1, source_target_pairs={{0,2},{1,3},{2,0},{3,1},{4,6},{5,7},{6,4},{7,5},{8,10},{9,11},{10,... | collective-permute-start | bytes 1769480 | tf_op jit(solution)/shard_map/ppermute | solution.py:46
  324.0 28.9 %collective-permute-start.52 = (bf16[4,240,384]{2,1,0:T(8,128)(2,1)S(1)}, bf16[4,240,384]{2,1,0:T(8,128)(2,1)S(1)}, u32[]{:S(2)}, u32[]{:S(2)}) collective-permute-start(bf16[4,240,384]{2,1,0:T(8,128)(2,1)S(1)} %pad_maximum_fusion.5), channel_id=1, source_target_pairs={{0,2},{1,3},{2,0},{3,1},{4,6},{5,7},{6,4},{7,5},{8,10},{9,11},{10,... | collective-permute-start | bytes 2211848 | tf_op jit(solution)/shard_map/ppermute | solution.py:46
  325.0 28.8 %collective-permute-start.50 = (bf16[4,240,384]{2,1,0:T(8,128)(2,1)S(1)}, bf16[4,240,384]{2,1,0:T(8,128)(2,1)S(1)}, u32[]{:S(2)}, u32[]{:S(2)}) collective-permute-start(bf16[4,240,384]{2,1,0:T(8,128)(2,1)S(1)} %pad_maximum_fusion.4), channel_id=1, source_target_pairs={{0,4},{1,5},{2,6},{3,7},{4,0},{5,1},{6,2},{7,3},{8,12},{9,13},{10,... | collective-permute-start | bytes 2211848 | tf_op jit(solution)/shard_map/ppermute | solution.py:46
  339.4 36.5 %collective-permute-start.68 = (bf16[4,192,768]{2,1,0:T(8,128)(2,1)}, bf16[4,192,768]{2,1,0:T(8,128)(2,1)}, u32[]{:S(2)}, u32[]{:S(2)}) collective-permute-start(bf16[4,192,768]{2,1,0:T(8,128)(2,1)} %pad_maximum_fusion.2), channel_id=1, source_target_pairs={{0,2},{1,3},{2,0},{3,1},{4,6},{5,7},{6,4},{7,5},{8,10},{9,11},{10,... | collective-permute-start | bytes 3538952 | tf_op jit(solution)/shard_map/ppermute | solution.py:46
  341.6 34.9 %collective-permute-start.66 = (bf16[4,192,768]{2,1,0:T(8,128)(2,1)}, bf16[4,192,768]{2,1,0:T(8,128)(2,1)}, u32[]{:S(2)}, u32[]{:S(2)}) collective-permute-start(bf16[4,192,768]{2,1,0:T(8,128)(2,1)} %pad_maximum_fusion.1), channel_id=1, source_target_pairs={{0,4},{1,5},{2,6},{3,7},{4,0},{5,1},{6,2},{7,3},{8,12},{9,13},{10,... | collective-permute-start | bytes 3538952 | tf_op jit(solution)/shard_map/ppermute | solution.py:46
  343.3 19.4 %collective-permute-start.63 = (bf16[192,384]{1,0:T(8,128)(2,1)}, bf16[192,384]{1,0:T(8,128)(2,1)}, u32[]{:S(2)}, u32[]{:S(2)}) collective-permute-start(bf16[192,384]{1,0:T(8,128)(2,1)} %select_bitcast_fusion.2), channel_id=1, source_target_pairs={{0,8},{1,9},{2,10},{3,11},{4,12},{5,13},{6,14},{7,15},{8,0},{9,1},... | collective-permute-start | bytes 442376 | tf_op jit(solution)/shard_map/ppermute | solution.py:46
  (87 other events, 733.1 us)
